TPU v7x, 32 devices: a whole 2x2x4 slice. The times are simulated.
32 devices in a mesh: row: 8 (over y, x, core), col: 4 (over z).
Axes of the slice: x: 2, y: 2, z: 4, core: 2. Of those that a mesh axis runs over, the one named last changes fastest.
Arguments:
- amplitudes: bfloat16 [256, 4096], P('row', 'col'), may hold values from -6 to 6
- integrals: bfloat16 [4096, 4096], P('col', 'row'), may hold values from -0.25 to 0.25
- occupied_irreps: int32 [256], replicated, may hold values from 0 to 7, as said below
- contracted_irreps: int32 [4096], P('col'), may hold values from 0 to 7
- output_irreps: int32 [4096], P('row'), may hold values from 0 to 7, as said below
Outputs:
- ladder: float32 [256, 4096], P('col', 'row')
Inputs may be any that keep to these rules, and one draw needn't show every extreme that they name: `occupied_irreps`: in each aligned block of 64 occupied pairs, every irrep appears exactly 64 // 8 times. `output_irreps`: in each aligned block of 512 output pairs, every irrep appears exactly 512 // 8 times.
All inputs are finite; a program needn't handle non-finite values.
Results may differ from a plain program's by a relative error of at most 0.0003.
Values may be sent and summed in bfloat16 or wider, within the bound.
No kernel may reach another device: no remote copies, remote signals or barrier semaphores. Data moves between devices by JAX's collectives and lax.ppermute only.
A program may use at most 64 MiB of HBM per device.

v0:
```python
import jax
import jax.numpy as jnp
from jax import lax
from jax.sharding import PartitionSpec as P


def body(amplitudes, integrals, occupied_irreps, contracted_irreps, output_irreps):
    col_count = lax.axis_size("col")
    pairs = occupied_irreps.shape[0]
    pair_share = pairs // col_count
    own_irreps = lax.dynamic_slice_in_dim(
        occupied_irreps, lax.axis_index("col") * pair_share, pair_share, 0
    )
    allowed = contracted_irreps[:, None] == output_irreps[None, :]
    masked = jnp.where(allowed, integrals, jnp.zeros_like(integrals))
    partial_sums = jnp.dot(
        lax.all_gather(amplitudes, "row", axis=0, tiled=True),
        masked,
        preferred_element_type=jnp.float32,
    )
    summed = lax.psum_scatter(partial_sums, "col", scatter_dimension=0, tiled=True)
    matches = own_irreps[:, None] == output_irreps[None, :]
    return jnp.where(matches, summed, jnp.zeros_like(summed))


def solution(mesh):
    return jax.shard_map(
        body,
        mesh=mesh,
        in_specs=(P("row", "col"), P("col", "row"), P(), P("col"), P("row")),
        out_specs=P("col", "row"),
        check_vma=False,
    )
```

profile of v0, /device:TPU:0, one launch (start us, length us, event | category | flops | bytes accessed | tf_op | source)
XLA Modules:
  0.0 52.0 jit_solution(14986923095626221347)
XLA Ops:
  6.5 0.0 reduce-scatter.4.cloned.1.call-start
  6.5 11.6 %all_gather.3 = bf16[256,1024]{1,0:T(8,128)(2,1)S(1)} all-gather(bf16[32,1024]{1,0:T(8,128)(2,1)} %param.5), channel_id=1, replica_groups=mesh['row'=8,'col'=4] {'row'}, dimensions={0}, use_global_device_ids=true | all-gather | bytes 589824 | tf_op jit(solution)/shard_map/all_gather | solution.py:17
  18.1 1.9 %convolution_bitcast_fusion = f32[256,512]{0,1:T(8,128)S(1)} fusion(bf16[256,1024]{1,0:T(8,128)(2,1)S(1)} %all_gather.3, bf16[1024,512]{1,0:T(8,128)(2,1)} %param.6, s32[512]{0:T(512)} %param.9, s32[1024]{0:T(1024)} %param.8), kind=kOutput, calls=%fused_computation.1 | convolution fusion | flops 269484032 | bytes 2103296 | tf_op jit(solution)/shard_map/dot_general | solution.py:16
  20.1 0.0 copy-start.1
  20.1 0.0 copy-start
  20.1 1.0 %copy.8 = f32[256,512]{1,0:T(8,128)} copy(f32[256,512]{0,1:T(8,128)S(1)} %convolution_bitcast_fusion) | data formatting | bytes 1048576
  21.1 0.0 reduce-scatter.4.cloned.1.call-update
  21.1 0.0 copy-done.1
  21.1 0.1 dynamic_slice.3
  21.2 22.0 %reduce-scatter.4.cloned.1.call-done = f32[64,512]{1,0:T(8,128)} async-done(((f32[256,512]{1,0:T(8,128)}), f32[64,512]{1,0:T(8,128)}) %reduce-scatter.4.cloned.1.call-update) | async-done | bytes 131088
  43.2 1.0 %copy.9 = f32[64,512]{0,1:T(8,128)S(1)} copy(f32[64,512]{1,0:T(8,128)} %reduce-scatter.4.cloned.1.call-done) | data formatting | bytes 262144
  44.2 0.0 copy-done
  44.2 0.1 compare_select_fusion.2
  44.4 0.8 %copy.7 = f32[64,512]{1,0:T(8,128)} copy(f32[64,512]{0,1:T(8,128)S(1)} %compare_select_fusion.2) | data formatting | bytes 262144 | tf_op jit(solution)/shard_map/jit(_where)/select_n | solution.py:23
Async XLA Ops:
  6.5 36.7 %reduce-scatter.4.cloned.1.call-start = ((), (), s32[]{:S(2)}) async-start(), calls=%async_computation.1 | async-start | bytes 655360
  20.1 1.1 %copy-start.1 = (s32[256]{0:T(256)S(1)}, s32[256]{0:T(256)}, u32[]{:S(2)}) copy-start(s32[256]{0:T(256)} %param.7) | copy-start | bytes 3076
  20.1 24.2 %copy-start = (s32[512]{0:T(512)S(1)}, s32[512]{0:T(512)}, u32[]{:S(2)}) copy-start(s32[512]{0:T(512)} %param.9) | copy-start | bytes 6148
Sparse Core Ops, SparseCore 0:
  21.2 21.9 reduce-scatter.3
where the time goes:
time: 52.2 us; the launch traced here: 52 us
  waiting for transfers between devices  22 us (42%)
  between operations  13.4 us (26%)
  blocking collectives  11.6 us (22%)
  local copies, waits for them, and re-layouts  2.88 us (6%)
  matrix products  1.93 us (4%)
    unnamed x2, waiting for transfers between devices  22 us
    all_gather x1, blocking collectives, body(): lax.all_gather(amplitudes, 'row', axis=0, tiled=True)  11.6 us
    unnamed x6, local copies, waits for them, and re-layouts  2.03 us
    dot_general x1, matrix products, body(): jnp.dot(lax.all_gather(amplitudes, 'row', axis=0, tiled=True), masked, pr...  1.93 us
  transfers between devices with their start and end apart: 1, of which 1 were waited for; matrix products, arithmetic and copies ran while one was open for 0% of the time, Pallas kernels for 0%

commit v1 on v0

--- a/solution.py
+++ b/solution.py
@@ -2,6 +2,24 @@
 import jax.numpy as jnp
 from jax import lax
 from jax.sharding import PartitionSpec as P
+
+
+def ring_gather(value, axis, dim):
+    ways, here, step = (lax.axis_size(axis), lax.axis_index(axis), value.shape[dim])
+    lengths = [n * ways if d == dim else n for d, n in enumerate(value.shape)]
+    full = lax.dynamic_update_slice_in_dim(
+        jnp.zeros(lengths, value.dtype), value, here * step, axis=dim
+    )
+    going_up = going_down = value
+    for far in range(1, ways // 2 + 1):
+        going_up = lax.ppermute(going_up, axis, [(d, (d + 1) % ways) for d in range(ways)])
+        full = lax.dynamic_update_slice_in_dim(full, going_up, (here - far) % ways * step, axis=dim)
+        if 2 * far < ways:
+            going_down = lax.ppermute(going_down, axis, [(d, (d - 1) % ways) for d in range(ways)])
+            full = lax.dynamic_update_slice_in_dim(
+                full, going_down, (here + far) % ways * step, axis=dim
+            )
+    return full
 
 
 def body(amplitudes, integrals, occupied_irreps, contracted_irreps, output_irreps):
@@ -14,9 +32,7 @@
     allowed = contracted_irreps[:, None] == output_irreps[None, :]
     masked = jnp.where(allowed, integrals, jnp.zeros_like(integrals))
     partial_sums = jnp.dot(
-        lax.all_gather(amplitudes, "row", axis=0, tiled=True),
-        masked,
-        preferred_element_type=jnp.float32,
+        ring_gather(amplitudes, "row", 0), masked, preferred_element_type=jnp.float32
     )
     summed = lax.psum_scatter(partial_sums, "col", scatter_dimension=0, tiled=True)
     matches = own_irreps[:, None] == output_irreps[None, :]

time: 52.2 us -> 59.5 us (1.14)
  blocking collectives: 11.6 us -> 0 us
  waiting for transfers between devices: 22 us -> 33 us
  starting transfers between devices: 0.01 us -> 8.72 us
  local copies, waits for them, and re-layouts: 2.88 us -> 1.07 us
  other arithmetic: 0.13 us -> 1.64 us
    reduce_scatter x0 -> x1, waiting for transfers between devices: none -> 23.4 us  [body(): lax.psum_scatter(partial_sums, 'col', scatter_dimension=0, tiled=True)]
    unnamed x2 -> x1, waiting for transfers between devices: 22 us -> 0.02 us
    all_gather x1 -> x0, blocking collectives: 11.6 us -> none  [body(): lax.all_gather(amplitudes, 'row', axis=0, tiled=True)]
    ppermute x0 -> x7, waiting for transfers between devices: none -> 9.57 us  [the longest x4 9.43 us: ring_gather(): lax.ppermute(going_up, axis, [(d, (d + 1) % ways) for d in range(ways)])]
    ppermute x0 -> x7, starting transfers between devices: none -> 8.72 us  [the longest x3 8.21 us: ring_gather(): lax.ppermute(going_down, axis, [(d, (d - 1) % ways) for d in range(ways)])]
    unnamed x6 -> x8, local copies, waits for them, and re-layouts: 2.03 us -> 0.02 us
    select_n x1, other arithmetic: 0.13 us -> 1.64 us  [body(): return jnp.where(matches, summed, jnp.zeros_like(summed))]
    dynamic_update_slice x0 -> x8, local copies, waits for them, and re-layouts: none -> 0.93 us  [the longest x1 0.86 us: ring_gather(): lax.dynamic_update_slice_in_dim(jnp.zeros(lengths, value.dtype), value, h...]
  transfers between devices with their start and end apart: 1 -> 8, of which waited for: 1 -> 6; matrix products, arithmetic and copies ran while one was open for 0% -> 2% of each run, Pallas kernels for 0% -> 0%
where the time goes in v1:
time: 59.5 us; the launch traced here: 59.3 us
  waiting for transfers between devices  33 us (55%)
  between operations  13.5 us (23%)
  starting transfers between devices  8.72 us (15%)
  other arithmetic  1.64 us (3%)
  matrix products  1.36 us (2%)
  local copies, waits for them, and re-layouts  1.07 us (2%)
    reduce_scatter x1, waiting for transfers between devices, body(): lax.psum_scatter(partial_sums, 'col', scatter_dimension=0, tiled=True)  23.4 us
    ppermute x4, waiting for transfers between devices, ring_gather(): lax.ppermute(going_up, axis, [(d, (d + 1) % ways) for d in range(ways)])  9.43 us
    ppermute x3, starting transfers between devices, ring_gather(): lax.ppermute(going_down, axis, [(d, (d - 1) % ways) for d in range(ways)])  8.21 us
    select_n x1, other arithmetic, body(): return jnp.where(matches, summed, jnp.zeros_like(summed))  1.64 us
    dot_general x1, matrix products, body(): jnp.dot(ring_gather(amplitudes, 'row', 0), masked, preferred_element_type...  1.36 us
  transfers between devices with their start and end apart: 8, of which 6 were waited for; matrix products, arithmetic and copies ran while one was open for 2% of the time, Pallas kernels for 0%

profile of v1, /device:TPU:0, one launch (start us, length us, event | category | flops | bytes accessed | tf_op | source)
XLA Modules:
  0.0 59.3 jit_solution(6653348136838585092)
XLA Ops:
  6.5 0.0 copy-start.1
  6.5 0.0 copy-start.2
  6.5 0.0 copy-start
  6.5 0.0 reduce-scatter.2.cloned.1.call-start
  6.5 0.5 collective-permute-start
  7.0 2.9 %collective-permute-start.1 = (bf16[32,1024]{1,0:T(8,128)(2,1)}, bf16[32,1024]{1,0:T(8,128)(2,1)S(1)}, u32[]{:S(2)}, u32[]{:S(2)}) collective-permute-start(bf16[32,1024]{1,0:T(8,128)(2,1)} %param.5), channel_id=1, source_target_pairs={{0,28},{4,0},{8,4},{12,8},{16,12},{20,16},{24,20},{28,24},{1,29},{... | collective-permute-start | bytes 196616 | tf_op jit(solution)/shard_map/ppermute | solution.py:18
  10.0 0.1 broadcast_in_dim.6
  10.1 0.9 %constant_dynamic-update-slice_fusion.7 = bf16[256,1024]{1,0:T(8,128)(2,1)S(1)} fusion(bf16[256,1024]{1,0:T(8,128)(2,1)S(1)} %broadcast_in_dim.6, bf16[32,1024]{1,0:T(8,128)(2,1)} %param.5, s32[]{:T(128)S(6)} %select_n.67), kind=kLoop, calls=%fused_computation.13 | loop fusion | bytes 131076 | tf_op jit(solution)/shard_map/dynamic_update_slice | solution.py:10
  10.9 1.2 %collective-permute-done = bf16[32,1024]{1,0:T(8,128)(2,1)S(1)} collective-permute-done((bf16[32,1024]{1,0:T(8,128)(2,1)}, bf16[32,1024]{1,0:T(8,128)(2,1)S(1)}, u32[]{:S(2)}, u32[]{:S(2)}) %collective-permute-start) | collective-permute-done | bytes 65568 | tf_op jit(solution)/shard_map/ppermute | solution.py:15
  12.1 0.0 collective-permute-start.2
  12.1 0.1 collective-permute-done.1
  12.2 2.6 %collective-permute-start.3 = (bf16[32,1024]{1,0:T(8,128)(2,1)S(1)}, bf16[32,1024]{1,0:T(8,128)(2,1)S(1)}, u32[]{:S(2)}, u32[]{:S(2)}) collective-permute-start(bf16[32,1024]{1,0:T(8,128)(2,1)S(1)} %collective-permute-done.1), channel_id=1, source_target_pairs={{0,28},{4,0},{8,4},{12,8},{16,12},{20,16},{24,20},{28,24},{1,29},{... | collective-permute-start | bytes 196616 | tf_op jit(solution)/shard_map/ppermute | solution.py:18
  14.8 1.9 %collective-permute-done.2 = bf16[32,1024]{1,0:T(8,128)(2,1)S(1)} collective-permute-done((bf16[32,1024]{1,0:T(8,128)(2,1)S(1)}, bf16[32,1024]{1,0:T(8,128)(2,1)S(1)}, u32[]{:S(2)}, u32[]{:S(2)}) %collective-permute-start.2) | collective-permute-done | bytes 65568 | tf_op jit(solution)/shard_map/ppermute | solution.py:15
  16.7 0.0 collective-permute-start.4
  16.7 0.0 collective-permute-done.3
  16.7 2.7 %collective-permute-start.5 = (bf16[32,1024]{1,0:T(8,128)(2,1)S(1)}, bf16[32,1024]{1,0:T(8,128)(2,1)S(1)}, u32[]{:S(2)}, u32[]{:S(2)}) collective-permute-start(bf16[32,1024]{1,0:T(8,128)(2,1)S(1)} %collective-permute-done.3), channel_id=1, source_target_pairs={{0,28},{4,0},{8,4},{12,8},{16,12},{20,16},{24,20},{28,24},{1,29},{... | collective-permute-start | bytes 196616 | tf_op jit(solution)/shard_map/ppermute | solution.py:18
  19.4 1.9 %collective-permute-done.4 = bf16[32,1024]{1,0:T(8,128)(2,1)S(1)} collective-permute-done((bf16[32,1024]{1,0:T(8,128)(2,1)S(1)}, bf16[32,1024]{1,0:T(8,128)(2,1)S(1)}, u32[]{:S(2)}, u32[]{:S(2)}) %collective-permute-start.4) | collective-permute-done | bytes 65568 | tf_op jit(solution)/shard_map/ppermute | solution.py:15
  21.3 0.0 collective-permute-start.6
  21.3 0.0 collective-permute-done.5
  21.3 4.5 %collective-permute-done.6 = bf16[32,1024]{1,0:T(8,128)(2,1)S(1)} collective-permute-done((bf16[32,1024]{1,0:T(8,128)(2,1)S(1)}, bf16[32,1024]{1,0:T(8,128)(2,1)S(1)}, u32[]{:S(2)}, u32[]{:S(2)}) %collective-permute-start.6) | collective-permute-done | bytes 65568 | tf_op jit(solution)/shard_map/ppermute | solution.py:15
  25.9 0.0 copy-done.1
  25.9 0.0 copy-done.2
  25.9 0.0 copy-done
  25.9 0.0 copy-start.3
  25.9 1.4 %fusion = f32[256,512]{1,0:T(8,128)} fusion(bf16[256,1024]{1,0:T(8,128)(2,1)S(1)} %constant_dynamic-update-slice_fusion, bf16[1024,512]{1,0:T(8,128)(2,1)S(1)} %copy-done.1, s32[512]{0:T(512)S(1)} %copy-done, s32[1024]{0:T(1024)S(1)} %copy-done.2), kind=kOutput, calls=%fused_computation.1 | convolution fusion | flops 269484032 | bytes 2103296 | tf_op jit(solution)/shard_map/dot_general | solution.py:34
  27.3 0.0 reduce-scatter.2.cloned.1.call-update
  27.3 0.0 copy-done.3
  27.3 0.1 dynamic_slice.3
  27.4 23.4 %reduce-scatter.2.cloned.1.call-done = f32[64,512]{1,0:T(8,128)} async-done(((f32[256,512]{1,0:T(8,128)}), f32[64,512]{1,0:T(8,128)}) %reduce-scatter.2.cloned.1.call-update) | async-done | bytes 131088 | tf_op jit(solution)/shard_map/reduce_scatter | solution.py:37
  50.8 1.6 %compare_select_fusion.2 = f32[64,512]{1,0:T(8,128)} fusion(f32[64,512]{1,0:T(8,128)} %reduce-scatter.2.cloned.1.call-done, s32[512]{0:T(512)S(1)} %copy-done, s32[64]{0:T(128)S(1)} %dynamic_slice.3), kind=kLoop, calls=%fused_computation.5 | loop fusion | flops 65536 | bytes 264448 | tf_op jit(solution)/shard_map/jit(_where)/select_n | solution.py:39
  (7 shorter events, 0.1 us)
Async XLA Ops:
  6.5 19.3 %copy-start.1 = (bf16[1024,512]{1,0:T(8,128)(2,1)S(1)}, bf16[1024,512]{1,0:T(8,128)(2,1)}, u32[]{:S(2)}) copy-start(bf16[1024,512]{1,0:T(8,128)(2,1)} %param.6) | copy-start | bytes 3145732
  6.5 19.3 %copy-start.2 = (s32[1024]{0:T(1024)S(1)}, s32[1024]{0:T(1024)}, u32[]{:S(2)}) copy-start(s32[1024]{0:T(1024)} %param.8) | copy-start | bytes 12292
  6.5 19.4 %copy-start = (s32[512]{0:T(512)S(1)}, s32[512]{0:T(512)}, u32[]{:S(2)}) copy-start(s32[512]{0:T(512)} %param.9) | copy-start | bytes 6148
  6.5 44.3 %reduce-scatter.2.cloned.1.call-start = ((), (), s32[]{:S(2)}) async-start(), calls=%async_computation.1 | async-start | bytes 655360 | tf_op jit(solution)/shard_map/reduce_scatter | solution.py:37
  6.5 5.5 %collective-permute-start = (bf16[32,1024]{1,0:T(8,128)(2,1)}, bf16[32,1024]{1,0:T(8,128)(2,1)S(1)}, u32[]{:S(2)}, u32[]{:S(2)}) collective-permute-start(bf16[32,1024]{1,0:T(8,128)(2,1)} %param.5), channel_id=1, source_target_pairs={{0,4},{4,8},{8,12},{12,16},{16,20},{20,24},{24,28},{28,0},{1,5},{5... | collective-permute-start | bytes 196616 | tf_op jit(solution)/shard_map/ppermute | solution.py:15
  7.0 5.2 %collective-permute-start.1 = (bf16[32,1024]{1,0:T(8,128)(2,1)}, bf16[32,1024]{1,0:T(8,128)(2,1)S(1)}, u32[]{:S(2)}, u32[]{:S(2)}) collective-permute-start(bf16[32,1024]{1,0:T(8,128)(2,1)} %param.5), channel_id=1, source_target_pairs={{0,28},{4,0},{8,4},{12,8},{16,12},{20,16},{24,20},{28,24},{1,29},{... | collective-permute-start | bytes 196616 | tf_op jit(solution)/shard_map/ppermute | solution.py:18
  12.1 4.6 %collective-permute-start.2 = (bf16[32,1024]{1,0:T(8,128)(2,1)S(1)}, bf16[32,1024]{1,0:T(8,128)(2,1)S(1)}, u32[]{:S(2)}, u32[]{:S(2)}) collective-permute-start(bf16[32,1024]{1,0:T(8,128)(2,1)S(1)} %collective-permute-done), channel_id=1, source_target_pairs={{0,4},{4,8},{8,12},{12,16},{16,20},{20,24},{24,28},{28,0},{1,5},{5... | collective-permute-start | bytes 196616 | tf_op jit(solution)/shard_map/ppermute | solution.py:15
  12.2 4.5 %collective-permute-start.3 = (bf16[32,1024]{1,0:T(8,128)(2,1)S(1)}, bf16[32,1024]{1,0:T(8,128)(2,1)S(1)}, u32[]{:S(2)}, u32[]{:S(2)}) collective-permute-start(bf16[32,1024]{1,0:T(8,128)(2,1)S(1)} %collective-permute-done.1), channel_id=1, source_target_pairs={{0,28},{4,0},{8,4},{12,8},{16,12},{20,16},{24,20},{28,24},{1,29},{... | collective-permute-start | bytes 196616 | tf_op jit(solution)/shard_map/ppermute | solution.py:18
  16.7 4.6 %collective-permute-start.4 = (bf16[32,1024]{1,0:T(8,128)(2,1)S(1)}, bf16[32,1024]{1,0:T(8,128)(2,1)S(1)}, u32[]{:S(2)}, u32[]{:S(2)}) collective-permute-start(bf16[32,1024]{1,0:T(8,128)(2,1)S(1)} %collective-permute-done.2), channel_id=1, source_target_pairs={{0,4},{4,8},{8,12},{12,16},{16,20},{20,24},{24,28},{28,0},{1,5},{5... | collective-permute-start | bytes 196616 | tf_op jit(solution)/shard_map/ppermute | solution.py:15
  16.7 4.6 %collective-permute-start.5 = (bf16[32,1024]{1,0:T(8,128)(2,1)S(1)}, bf16[32,1024]{1,0:T(8,128)(2,1)S(1)}, u32[]{:S(2)}, u32[]{:S(2)}) collective-permute-start(bf16[32,1024]{1,0:T(8,128)(2,1)S(1)} %collective-permute-done.3), channel_id=1, source_target_pairs={{0,28},{4,0},{8,4},{12,8},{16,12},{20,16},{24,20},{28,24},{1,29},{... | collective-permute-start | bytes 196616 | tf_op jit(solution)/shard_map/ppermute | solution.py:18
  21.3 4.6 %collective-permute-start.6 = (bf16[32,1024]{1,0:T(8,128)(2,1)S(1)}, bf16[32,1024]{1,0:T(8,128)(2,1)S(1)}, u32[]{:S(2)}, u32[]{:S(2)}) collective-permute-start(bf16[32,1024]{1,0:T(8,128)(2,1)S(1)} %collective-permute-done.4), channel_id=1, source_target_pairs={{0,4},{4,8},{8,12},{12,16},{16,20},{20,24},{24,28},{28,0},{1,5},{5... | collective-permute-start | bytes 196616 | tf_op jit(solution)/shard_map/ppermute | solution.py:15
  25.9 1.4 %copy-start.3 = (s32[256]{0:T(256)S(1)}, s32[256]{0:T(256)}, u32[]{:S(2)}) copy-start(s32[256]{0:T(256)} %param.7) | copy-start | bytes 3076
Sparse Core Ops, SparseCore 0:
  27.4 23.3 reduce-scatter.1
